TPU v7x, 32 devices: a whole 2x2x4 slice. The times are simulated.
32 devices in a mesh: dp: 8 (over z, core), tensor: 4 (over y, x).
Axes of the slice: x: 2, y: 2, z: 4, core: 2. Of those that a mesh axis runs over, the one named last changes fastest.
Arguments:
- tokens: bfloat16 [8192, 2048], P(('dp', 'tensor')), may hold values from -6 to 6
- lengths: int32 [8, 3], P('dp'), may hold values from 1 to 512, 768 in all within a row
- query_weight: bfloat16 [2048, 2048], P('dp', 'tensor'), may hold values from -0.125 to 0.125
- key_weight: bfloat16 [2048, 2048], P('dp', 'tensor'), may hold values from -0.125 to 0.125
- value_weight: bfloat16 [2048, 2048], P('dp', 'tensor'), may hold values from -0.125 to 0.125
- output_weight: bfloat16 [2048, 2048], P('tensor', 'dp'), may hold values from -1.5 to 1.5
- gate_weight: bfloat16 [2048, 8192], P('dp', 'tensor'), may hold values from -0.125 to 0.125
- up_weight: bfloat16 [2048, 8192], P('dp', 'tensor'), may hold values from -0.125 to 0.125
- down_weight: bfloat16 [8192, 2048], P('tensor', 'dp'), may hold values from -0.0625 to 0.0625
- cotangent: bfloat16 [8192, 2048], P(('dp', 'tensor')), may hold values from -6 to 6
Outputs:
- output: bfloat16 [8192, 2048], P(('dp', 'tensor'))
- input_grad: bfloat16 [8192, 2048], P(('dp', 'tensor'))
- query_grad: float32 [2048, 2048], P('dp', 'tensor')
- key_grad: float32 [2048, 2048], P('dp', 'tensor')
- value_grad: float32 [2048, 2048], P('dp', 'tensor')
- output_grad: float32 [2048, 2048], P('tensor', 'dp')
- gate_grad: float32 [2048, 8192], P('dp', 'tensor')
- up_grad: float32 [2048, 8192], P('dp', 'tensor')
- down_grad: float32 [8192, 2048], P('tensor', 'dp')
Inputs may be any that keep to these rules, and one draw needn't show every extreme that they name: Each row holds the lengths of the 3 documents packed from the start of a slot of 1024 positions; the rest of the slot is padding. Every row's largest length is 512 and its lengths add to 768.
All inputs are finite; a program needn't handle non-finite values.
Results may differ from a plain program's by a relative error of at most 0.023.
Values may be sent and summed in bfloat16 or wider, within the bound.
No kernel may reach another device: no remote copies, remote signals or barrier semaphores. Data moves between devices by JAX's collectives and lax.ppermute only.
A program may use at most 256 MiB of HBM per device.

v0:
```python
import math
import jax
import jax.numpy as jnp
from jax import lax
from jax.sharding import PartitionSpec as P

HD = 128
QBLOCK = 512
EPSILON = 1e-05
ROPE_BASE = 10000.0
MASKED = -1e30


def layer_norm(rows):
    centre = jnp.mean(rows, axis=-1, keepdims=True)
    centered = rows - centre
    spread = jnp.mean(centered * centered, axis=-1, keepdims=True)
    return centered * lax.rsqrt(spread + EPSILON)


def slot_layout(lengths_row, row_total):
    ends = jnp.cumsum(lengths_row)
    places = jnp.arange(row_total, dtype=jnp.int32)
    segment = jnp.sum((places[:, None] >= ends[None, :]).astype(jnp.int32), axis=1)
    starts = jnp.concatenate([jnp.zeros((1,), jnp.int32), ends])
    picks = jnp.arange(starts.shape[0], dtype=jnp.int32)
    begins = jnp.sum(jnp.where(segment[:, None] == picks[None, :], starts[None, :], 0), axis=1)
    position = places - begins
    valid = (places < ends[-1]).astype(jnp.int32)
    return (segment, position, places, valid)


def rope_tables(position, head_size):
    half_size = head_size // 2
    steps_float = jnp.arange(half_size, dtype=jnp.float32)
    freqs = jnp.exp(steps_float * (-2.0 * math.log(ROPE_BASE) / head_size))
    angles = position.astype(jnp.float32)[:, None] * freqs[None, :]
    return (jnp.cos(angles), jnp.sin(angles))


def rotate(values, cosine_table, sine_table):
    half_size = values.shape[-1] // 2
    first_half = values[..., :half_size]
    second_half = values[..., half_size:]
    cosine_wide = cosine_table[:, None, :]
    sine_wide = sine_table[:, None, :]
    return jnp.concatenate(
        [
            first_half * cosine_wide - second_half * sine_wide,
            second_half * cosine_wide + first_half * sine_wide,
        ],
        axis=-1,
    )


def swish_product(gate_pre, up_pre):
    return jax.nn.silu(gate_pre) * up_pre


def dot_first(left, right):
    return lax.dot_general(
        left, right, (((0,), (0,)), ((), ())), preferred_element_type=jnp.float32
    )


def dot_last(left, right):
    return lax.dot_general(
        left, right, (((1,), (1,)), ((), ())), preferred_element_type=jnp.float32
    )


def block_scores(queries, keys_turned, segment_rows, segment_cols, place_rows, place_cols, scale):
    raw_scores = (
        jnp.einsum("qhd,khd->hqk", queries, keys_turned, preferred_element_type=jnp.float32) * scale
    )
    allowed = (segment_rows[:, None] == segment_cols[None, :]) & (
        place_rows[:, None] >= place_cols[None, :]
    )
    return jnp.where(allowed[None], raw_scores, MASKED)


def attend_forward(queries, keys_turned, values, segment, places, block_rows):
    slot_rows = queries.shape[0]
    scale = queries.shape[2] ** (-0.5)
    context_blocks = []
    log_totals = []
    for block_index in range(slot_rows // block_rows):
        lower_row = block_index * block_rows
        reach_row = lower_row + block_rows
        scores = block_scores(
            queries[lower_row:reach_row],
            keys_turned[:reach_row],
            segment[lower_row:reach_row],
            segment[:reach_row],
            places[lower_row:reach_row],
            places[:reach_row],
            scale,
        )
        row_peak = jnp.max(scores, axis=-1, keepdims=True)
        weights = jnp.exp(scores - row_peak)
        row_total = jnp.sum(weights, axis=-1, keepdims=True)
        probs = (weights / row_total).astype(jnp.bfloat16)
        context_blocks.append(
            jnp.einsum(
                "hqk,khd->qhd", probs, values[:reach_row], preferred_element_type=jnp.float32
            ).astype(jnp.bfloat16)
        )
        log_totals.append(row_peak + jnp.log(row_total))
    return (jnp.concatenate(context_blocks, axis=0), log_totals)


def attend_backward(
    queries, keys_turned, values, segment, places, log_totals, d_context, block_rows
):
    slot_rows, heads_here, head_size = queries.shape
    scale = head_size ** (-0.5)
    d_keys = jnp.zeros((slot_rows, heads_here, head_size), jnp.float32)
    d_values = jnp.zeros((slot_rows, heads_here, head_size), jnp.float32)
    d_query_blocks = []
    for block_index in range(slot_rows // block_rows):
        lower_row = block_index * block_rows
        reach_row = lower_row + block_rows
        query_block = queries[lower_row:reach_row]
        scores = block_scores(
            query_block,
            keys_turned[:reach_row],
            segment[lower_row:reach_row],
            segment[:reach_row],
            places[lower_row:reach_row],
            places[:reach_row],
            scale,
        )
        probs = jnp.exp(scores - log_totals[block_index])
        grads_block = d_context[lower_row:reach_row]
        d_probs = jnp.einsum(
            "qhd,khd->hqk", grads_block, values[:reach_row], preferred_element_type=jnp.float32
        )
        inner = jnp.sum(probs * d_probs, axis=-1, keepdims=True)
        d_scores = (probs * (d_probs - inner) * scale).astype(jnp.bfloat16)
        d_query_blocks.append(
            jnp.einsum(
                "hqk,khd->qhd",
                d_scores,
                keys_turned[:reach_row],
                preferred_element_type=jnp.float32,
            )
        )
        d_keys = d_keys.at[:reach_row].add(
            jnp.einsum("hqk,qhd->khd", d_scores, query_block, preferred_element_type=jnp.float32)
        )
        d_values = d_values.at[:reach_row].add(
            jnp.einsum(
                "hqk,qhd->khd",
                probs.astype(jnp.bfloat16),
                grads_block,
                preferred_element_type=jnp.float32,
            )
        )
    return (jnp.concatenate(d_query_blocks, axis=0), d_keys, d_values)


def per_device(
    tokens,
    lengths,
    query_weight,
    key_weight,
    value_weight,
    output_weight,
    gate_weight,
    up_weight,
    down_weight,
    cotangent,
):
    row_count = tokens.shape[0]
    slot_rows = row_count * lax.axis_size("tensor")
    first_row = lax.axis_index("tensor") * row_count
    segment, position, places, valid_all = slot_layout(lengths[0], slot_rows)
    valid_rows = lax.dynamic_slice_in_dim(valid_all, first_row, row_count, 0).astype(jnp.float32)[
        :, None
    ]
    cosine_table, sine_table = rope_tables(position, HD)
    heads_here = query_weight.shape[1] // HD
    weights = (
        lax.all_gather(query_weight, "dp", axis=0, tiled=True),
        lax.all_gather(key_weight, "dp", axis=0, tiled=True),
        lax.all_gather(value_weight, "dp", axis=0, tiled=True),
        lax.all_gather(output_weight, "dp", axis=1, tiled=True),
        lax.all_gather(gate_weight, "dp", axis=0, tiled=True),
        lax.all_gather(up_weight, "dp", axis=0, tiled=True),
        lax.all_gather(down_weight, "dp", axis=1, tiled=True),
    )
    residual_in = tokens.astype(jnp.float32)
    normed_one = layer_norm(residual_in).astype(jnp.bfloat16)
    gathered_one = lax.all_gather(normed_one, "tensor", axis=0, tiled=True)
    query_pre = jnp.dot(gathered_one, weights[0], preferred_element_type=jnp.float32).reshape(
        slot_rows, heads_here, HD
    )
    key_pre = jnp.dot(gathered_one, weights[1], preferred_element_type=jnp.float32).reshape(
        slot_rows, heads_here, HD
    )
    values = (
        jnp.dot(gathered_one, weights[2], preferred_element_type=jnp.float32)
        .astype(jnp.bfloat16)
        .reshape(slot_rows, heads_here, HD)
    )
    queries = rotate(query_pre, cosine_table, sine_table).astype(jnp.bfloat16)
    keys_turned = rotate(key_pre, cosine_table, sine_table).astype(jnp.bfloat16)
    context, log_totals = attend_forward(queries, keys_turned, values, segment, places, QBLOCK)
    context_flat = context.reshape(slot_rows, heads_here * HD)
    picked = context_flat
    attention_out = lax.psum_scatter(
        jnp.dot(picked, weights[3], preferred_element_type=jnp.float32).astype(jnp.bfloat16),
        "tensor",
        scatter_dimension=0,
        tiled=True,
    ).astype(jnp.float32)
    middle = residual_in + attention_out
    normed_two = layer_norm(middle).astype(jnp.bfloat16)
    gathered_two = lax.all_gather(normed_two, "tensor", axis=0, tiled=True)
    gate_pre = jnp.dot(gathered_two, weights[4], preferred_element_type=jnp.float32)
    up_pre = jnp.dot(gathered_two, weights[5], preferred_element_type=jnp.float32)
    hidden = swish_product(gate_pre, up_pre).astype(jnp.bfloat16)
    picked = hidden
    feed_out = lax.psum_scatter(
        jnp.dot(picked, weights[6], preferred_element_type=jnp.float32).astype(jnp.bfloat16),
        "tensor",
        scatter_dimension=0,
        tiled=True,
    ).astype(jnp.float32)
    output = (valid_rows * (middle + feed_out)).astype(jnp.bfloat16)
    weights = (
        lax.all_gather(query_weight, "dp", axis=0, tiled=True),
        lax.all_gather(key_weight, "dp", axis=0, tiled=True),
        lax.all_gather(value_weight, "dp", axis=0, tiled=True),
        lax.all_gather(output_weight, "dp", axis=1, tiled=True),
        lax.all_gather(gate_weight, "dp", axis=0, tiled=True),
        lax.all_gather(up_weight, "dp", axis=0, tiled=True),
        lax.all_gather(down_weight, "dp", axis=1, tiled=True),
    )
    masked_grad = valid_rows * cotangent.astype(jnp.float32)
    feed_grad = masked_grad.astype(jnp.bfloat16)
    rows_piece = lax.all_gather(feed_grad, "tensor", axis=0, tiled=True)
    picked = hidden
    down_part = dot_first(picked, rows_piece)
    hidden_part = dot_last(rows_piece, weights[6])
    _, swish_pull = jax.vjp(swish_product, gate_pre, up_pre)
    d_gate, d_up = swish_pull(hidden_part)
    d_gate = d_gate.astype(jnp.bfloat16)
    d_up = d_up.astype(jnp.bfloat16)
    gate_local = dot_first(gathered_two, d_gate)
    up_local = dot_first(gathered_two, d_up)
    d_normed_two = lax.psum_scatter(
        (dot_last(d_gate, weights[4]) + dot_last(d_up, weights[5])).astype(jnp.bfloat16),
        "tensor",
        scatter_dimension=0,
        tiled=True,
    ).astype(jnp.float32)
    _, second_pull = jax.vjp(layer_norm, middle)
    d_middle = masked_grad + second_pull(d_normed_two)[0]
    attention_grad = d_middle.astype(jnp.bfloat16)
    rows_piece = lax.all_gather(attention_grad, "tensor", axis=0, tiled=True)
    picked = context_flat
    weight_part = dot_first(picked, rows_piece)
    context_part = dot_last(rows_piece, weights[3])
    d_context = context_part
    d_context = d_context.astype(jnp.bfloat16).reshape(slot_rows, heads_here, HD)
    d_queries, d_keys, d_values = attend_backward(
        queries, keys_turned, values, segment, places, log_totals, d_context, QBLOCK
    )
    _, turn_pull = jax.vjp(lambda moved: rotate(moved, cosine_table, sine_table), query_pre)
    d_query_pre = turn_pull(d_queries)[0].astype(jnp.bfloat16).reshape(slot_rows, heads_here * HD)
    d_key_pre = turn_pull(d_keys)[0].astype(jnp.bfloat16).reshape(slot_rows, heads_here * HD)
    d_value_pre = d_values.astype(jnp.bfloat16).reshape(slot_rows, heads_here * HD)
    query_local = dot_first(gathered_one, d_query_pre)
    key_local = dot_first(gathered_one, d_key_pre)
    value_local = dot_first(gathered_one, d_value_pre)
    d_normed_one = lax.psum_scatter(
        (
            dot_last(d_query_pre, weights[0])
            + dot_last(d_key_pre, weights[1])
            + dot_last(d_value_pre, weights[2])
        ).astype(jnp.bfloat16),
        "tensor",
        scatter_dimension=0,
        tiled=True,
    ).astype(jnp.float32)
    _, first_pull = jax.vjp(layer_norm, residual_in)
    input_grad = (d_middle + first_pull(d_normed_one)[0]).astype(jnp.bfloat16)
    query_sum, key_sum, value_sum, output_sum, gate_sum, up_sum, down_sum = (
        lax.psum_scatter(
            query_local.astype(jnp.bfloat16), "dp", scatter_dimension=0, tiled=True
        ).astype(jnp.float32),
        lax.psum_scatter(
            key_local.astype(jnp.bfloat16), "dp", scatter_dimension=0, tiled=True
        ).astype(jnp.float32),
        lax.psum_scatter(
            value_local.astype(jnp.bfloat16), "dp", scatter_dimension=0, tiled=True
        ).astype(jnp.float32),
        lax.psum_scatter(
            weight_part.astype(jnp.bfloat16), "dp", scatter_dimension=1, tiled=True
        ).astype(jnp.float32),
        lax.psum_scatter(
            gate_local.astype(jnp.bfloat16), "dp", scatter_dimension=0, tiled=True
        ).astype(jnp.float32),
        lax.psum_scatter(
            up_local.astype(jnp.bfloat16), "dp", scatter_dimension=0, tiled=True
        ).astype(jnp.float32),
        lax.psum_scatter(
            down_part.astype(jnp.bfloat16), "dp", scatter_dimension=1, tiled=True
        ).astype(jnp.float32),
    )
    return (
        output,
        input_grad,
        query_sum,
        key_sum,
        value_sum,
        output_sum,
        gate_sum,
        up_sum,
        down_sum,
    )


def solution(mesh):
    return jax.shard_map(
        per_device,
        mesh=mesh,
        in_specs=(
            P(("dp", "tensor"), None),
            P("dp", None),
            P("dp", "tensor"),
            P("dp", "tensor"),
            P("dp", "tensor"),
            P("tensor", "dp"),
            P("dp", "tensor"),
            P("dp", "tensor"),
            P("tensor", "dp"),
            P(("dp", "tensor"), None),
        ),
        out_specs=(
            P(("dp", "tensor"), None),
            P(("dp", "tensor"), None),
            P("dp", "tensor"),
            P("dp", "tensor"),
            P("dp", "tensor"),
            P("tensor", "dp"),
            P("dp", "tensor"),
            P("dp", "tensor"),
            P("tensor", "dp"),
        ),
        check_vma=False,
    )
```

profile of v0, /device:TPU:0, one launch (start us, length us, event | category | flops | bytes accessed | tf_op | source)
XLA Modules:
  0.0 1302.9 jit_solution(14232833161550070507)
XLA Ops:
  22.0 19.5 %all-gather.18.cloned.1.call-done = bf16[2048,512]{1,0:T(8,128)(2,1)} async-done(((bf16[256,512]{1,0:T(8,128)(2,1)}), bf16[2048,512]{1,0:T(8,128)(2,1)}) %all-gather.18.cloned.1.call-update) | async-done | bytes 2097168 | tf_op jit(solution)/shard_map/all_gather | solution.py:185
  41.5 54.4 %all-gather.12.cloned.1.call-done = bf16[1024,2048]{1,0:T(8,128)(2,1)} async-done(((bf16[256,2048]{1,0:T(8,128)(2,1)}), bf16[1024,2048]{1,0:T(8,128)(2,1)}) %all-gather.12.cloned.1.call-update) | async-done | bytes 4194320 | tf_op jit(solution)/shard_map/all_gather | solution.py:194
  105.2 21.5 %all-gather.16.cloned.1.call-done = bf16[2048,512]{1,0:T(8,128)(2,1)} async-done(((bf16[256,512]{1,0:T(8,128)(2,1)}), bf16[2048,512]{1,0:T(8,128)(2,1)}) %all-gather.16.cloned.1.call-update) | async-done | bytes 2097168 | tf_op jit(solution)/shard_map/all_gather | solution.py:184
  143.5 13.3 %all-gather.14.cloned.1.call-done = bf16[2048,512]{1,0:T(8,128)(2,1)} async-done(((bf16[256,512]{1,0:T(8,128)(2,1)}), bf16[2048,512]{1,0:T(8,128)(2,1)}) %all-gather.14.cloned.1.call-update) | async-done | bytes 2097168 | tf_op jit(solution)/shard_map/all_gather | solution.py:186
  174.7 13.5 %all-gather.20.cloned.1.call-done = bf16[512,2048]{1,0:T(8,128)(2,1)} async-done(((bf16[512,256]{1,0:T(8,128)(2,1)}), bf16[512,2048]{1,0:T(8,128)(2,1)}) %all-gather.20.cloned.1.call-update) | async-done | bytes 2097168 | tf_op jit(solution)/shard_map/all_gather | solution.py:187
  195.0 51.0 %reduce-scatter.12.cloned.1.call-done = bf16[256,2048]{1,0:T(8,128)(2,1)} async-done(((bf16[1024,2048]{1,0:T(8,128)(2,1)}), bf16[256,2048]{1,0:T(8,128)(2,1)}) %reduce-scatter.12.cloned.1.call-update) | async-done | bytes 1048592 | tf_op jit(solution)/shard_map/reduce_scatter | solution.py:211
  255.1 74.6 %all-gather.26.cloned.1.call-done = bf16[2048,2048]{1,0:T(8,128)(2,1)} async-done(((bf16[256,2048]{1,0:T(8,128)(2,1)}), bf16[2048,2048]{1,0:T(8,128)(2,1)}) %all-gather.26.cloned.1.call-update) | async-done | bytes 8388624 | tf_op jit(solution)/shard_map/all_gather | solution.py:189
  329.7 53.5 %all-gather.22.cloned.1.call-done = bf16[1024,2048]{1,0:T(8,128)(2,1)} async-done(((bf16[256,2048]{1,0:T(8,128)(2,1)}), bf16[1024,2048]{1,0:T(8,128)(2,1)}) %all-gather.22.cloned.1.call-update) | async-done | bytes 4194320 | tf_op jit(solution)/shard_map/all_gather | solution.py:219
  383.2 14.8 %fusion.133 = f32[1024,2048]{1,0:T(8,128)} fusion(bf16[1024,2048]{1,0:T(8,128)(2,1)} %all-gather.22.cloned.1.call-done, bf16[2048,2048]{1,0:T(8,128)(2,1)} %all-gather.26.cloned.1.call-done), kind=kOutput, calls=%fused_computation.177 | convolution fusion | flops 8589934592 | bytes 20971520 | tf_op jit(solution)/shard_map/dot_general | solution.py:221
  398.0 68.9 %all-gather.24.cloned.1.call-done = bf16[2048,2048]{1,0:T(8,128)(2,1)} async-done(((bf16[256,2048]{1,0:T(8,128)(2,1)}), bf16[2048,2048]{1,0:T(8,128)(2,1)}) %all-gather.24.cloned.1.call-update) | async-done | bytes 8388624 | tf_op jit(solution)/shard_map/all_gather | solution.py:188
  466.9 14.4 %fusion.132 = f32[1024,2048]{1,0:T(8,128)} fusion(bf16[1024,2048]{1,0:T(8,128)(2,1)} %all-gather.22.cloned.1.call-done, bf16[2048,2048]{1,0:T(8,128)(2,1)} %all-gather.24.cloned.1.call-done), kind=kOutput, calls=%fused_computation.176 | convolution fusion | flops 8589934592 | bytes 20971520 | tf_op jit(solution)/shard_map/dot_general | solution.py:220
  481.3 39.0 %all-gather.30.cloned.1.call-done = bf16[1024,2048]{1,0:T(8,128)(2,1)} async-done(((bf16[256,2048]{1,0:T(8,128)(2,1)}), bf16[1024,2048]{1,0:T(8,128)(2,1)}) %all-gather.30.cloned.1.call-update) | async-done | bytes 4194320 | tf_op jit(solution)/shard_map/all_gather | solution.py:242
  520.3 84.1 %all-gather.28.cloned.1.call-done = bf16[2048,2048]{1,0:T(8,128)(2,1)} async-done(((bf16[2048,256]{1,0:T(8,128)(2,1)}), bf16[2048,2048]{1,0:T(8,128)(2,1)}) %all-gather.28.cloned.1.call-update) | async-done | bytes 8388624 | tf_op jit(solution)/shard_map/all_gather | solution.py:190
  604.4 21.7 %multiply_convert_fusion.1 = (bf16[1024,2048]{1,0:T(8,128)(2,1)}, bf16[1024,2048]{1,0:T(8,128)(2,1)}, bf16[1024,2048]{1,0:T(8,128)(2,1)}) fusion(f32[1024,2048]{1,0:T(8,128)} %fusion.132, f32[1024,2048]{1,0:T(8,128)} %fusion.133, bf16[1024,2048]{1,0:T(8,128)(2,1)} %all-gather.30.cloned.1.call-done, bf16[2048,2048]{1,0:T(8,128)(2,1)} %all-gather.28.cloned.1.call-done), kind=kOutput, calls=%fused_computation.12 | convolution fusion | flops 8623489024 | bytes 41943040 | tf_op jit(solution)/shard_map/dot_general | solution.py:67
  626.1 12.9 fusion.134
  639.0 12.9 add_convert_fusion.1
  652.0 50.9 %reduce-scatter.16.cloned.1.call-done = bf16[256,2048]{1,0:T(8,128)(2,1)} async-done(((bf16[1024,2048]{1,0:T(8,128)(2,1)}), bf16[256,2048]{1,0:T(8,128)(2,1)}) %reduce-scatter.16.cloned.1.call-update) | async-done | bytes 1048592 | tf_op jit(solution)/shard_map/reduce_scatter | solution.py:252
  709.4 14.4 %convolution_convert_fusion.1 = bf16[2048,2048]{1,0:T(8,128)(2,1)} fusion(bf16[1024,2048]{1,0:T(8,128)(2,1)} %all-gather.22.cloned.1.call-done, bf16[1024,2048]{1,0:T(8,128)(2,1)} %get-tuple-element.73), kind=kOutput, calls=%fused_computation.20 | convolution fusion | flops 8594128896 | bytes 16777216 | tf_op jit(solution)/shard_map/dot_general | solution.py:61
  723.8 14.1 %convolution_convert_fusion.2 = bf16[2048,2048]{1,0:T(8,128)(2,1)} fusion(bf16[1024,2048]{1,0:T(8,128)(2,1)} %all-gather.22.cloned.1.call-done, bf16[1024,2048]{1,0:T(8,128)(2,1)} %get-tuple-element.74), kind=kOutput, calls=%fused_computation.21 | convolution fusion | flops 8594128896 | bytes 16777216 | tf_op jit(solution)/shard_map/dot_general | solution.py:61
  738.0 14.3 %convolution_convert_fusion = bf16[2048,2048]{1,0:T(8,128)(2,1)} fusion(bf16[1024,2048]{1,0:T(8,128)(2,1)} %get-tuple-element.75, bf16[1024,2048]{1,0:T(8,128)(2,1)} %all-gather.30.cloned.1.call-done), kind=kOutput, calls=%fused_computation.19 | convolution fusion | flops 8594128896 | bytes 16777216 | tf_op jit(solution)/shard_map/dot_general | solution.py:61
  752.5 9.6 all-gather.32.cloned.1.call-done
  803.5 20.9 %fusion.89 = f32[512,4,128]{2,0,1:T(8,128)} fusion(f32[4,512,1024]{2,1,0:T(8,128)} %fusion.136, f32[4,512,1024]{2,1,0:T(8,128)} %copy-done.6, f32[4,512]{1,0:T(4,128)S(1)} %log_add_fusion, pred[512,1024]{1,0:T(8,128)(4,1)S(1)} %copy-done.20, bf16[1024,4,64]{2,0,1:T(8,128)(2,1)S(1)} %copy-done.13, bf16[1024,4,64]{2,0,1:T(8,128)(2,1)S(1)} %copy-done.11), kind=kOutput, calls=%fused_computation.113 | convolution fusion | flops 562039808 | bytes 19406848 | tf_op jit(solution)/shard_map/hqk,khd->qhd/dot_general | solution.py:141
  833.8 26.0 %bitcast_add_fusion.1 = f32[1024,4,128]{2,0,1:T(8,128)} fusion(f32[512,4,128]{2,0,1:T(8,128)S(1)} %copy-done.63, bf16[512,4,128]{2,0,1:T(8,128)(2,1)S(1)} %copy-done.25, f32[4,512,1024]{2,1,0:T(8,128)} %fusion.136, f32[4,512,1024]{2,1,0:T(8,128)} %copy-done.6, f32[4,512]{1,0:T(4,128)S(1)} %log_add_fusion, pred[512,1024]{1,0:T(8,128)(4,1)S(1)} %copy-done.20), kind=kOutput, calls=%fused_computation.79 | convolution fusion | flops 560466944 | bytes 20979712 | tf_op jit(solution)/shard_map/hqk,qhd->khd/dot_general | solution.py:149
  895.9 13.9 %convolution_convert_fusion.3 = bf16[1024,2048]{1,0:T(8,128)(2,1)} fusion(bf16[1024,2048]{1,0:T(8,128)(2,1)} %get-tuple-element.75, bf16[2048,2048]{1,0:T(8,128)(2,1)} %all-gather.28.cloned.1.call-done), kind=kOutput, calls=%fused_computation.48 | convolution fusion | flops 8592031744 | bytes 16777216 | tf_op jit(solution)/shard_map/dot_general | solution.py:225
  912.7 31.3 %reduce-scatter.28.cloned.1.call-done = bf16[256,2048]{1,0:T(8,128)(2,1)} async-done(((bf16[2048,2048]{1,0:T(8,128)(2,1)}), bf16[256,2048]{1,0:T(8,128)(2,1)}) %reduce-scatter.28.cloned.1.call-update) | async-done | bytes 1048592 | tf_op jit(solution)/shard_map/reduce_scatter | solution.py:302
  946.8 87.4 %reduce-scatter.32.cloned.1.call-done = bf16[2048,256]{1,0:T(8,128)(2,1)} async-done(((bf16[2048,2048]{1,0:T(8,128)(2,1)}), bf16[2048,256]{1,0:T(8,128)(2,1)}) %reduce-scatter.32.cloned.1.call-update) | async-done | bytes 1048592 | tf_op jit(solution)/shard_map/reduce_scatter | solution.py:308
  1036.9 34.0 %reduce-scatter.26.cloned.1.call-done = bf16[512,256]{1,0:T(8,128)(2,1)} async-done(((bf16[512,2048]{1,0:T(8,128)(2,1)}), bf16[512,256]{1,0:T(8,128)(2,1)}) %reduce-scatter.26.cloned.1.call-update) | async-done | bytes 262160 | tf_op jit(solution)/shard_map/reduce_scatter | solution.py:299
  1072.6 35.1 %reduce-scatter.24.cloned.1.call-done = bf16[256,512]{1,0:T(8,128)(2,1)} async-done(((bf16[2048,512]{1,0:T(8,128)(2,1)}), bf16[256,512]{1,0:T(8,128)(2,1)}) %reduce-scatter.24.cloned.1.call-update) | async-done | bytes 262160 | tf_op jit(solution)/shard_map/reduce_scatter | solution.py:296
  1109.5 35.2 %reduce-scatter.20.cloned.1.call-done = bf16[256,512]{1,0:T(8,128)(2,1)} async-done(((bf16[2048,512]{1,0:T(8,128)(2,1)}), bf16[256,512]{1,0:T(8,128)(2,1)}) %reduce-scatter.20.cloned.1.call-update) | async-done | bytes 262160 | tf_op jit(solution)/shard_map/reduce_scatter | solution.py:290
  1146.5 35.0 %reduce-scatter.22.cloned.1.call-done = bf16[256,512]{1,0:T(8,128)(2,1)} async-done(((bf16[2048,512]{1,0:T(8,128)(2,1)}), bf16[256,512]{1,0:T(8,128)(2,1)}) %reduce-scatter.22.cloned.1.call-update) | async-done | bytes 262160 | tf_op jit(solution)/shard_map/reduce_scatter | solution.py:293
  1183.3 52.4 %reduce-scatter.18.cloned.1.call-done = bf16[256,2048]{1,0:T(8,128)(2,1)} async-done(((bf16[1024,2048]{1,0:T(8,128)(2,1)}), bf16[256,2048]{1,0:T(8,128)(2,1)}) %reduce-scatter.18.cloned.1.call-update) | async-done | bytes 1048592 | tf_op jit(solution)/shard_map/reduce_scatter | solution.py:277
  1239.4 51.9 %reduce-scatter.14.cloned.1.call-done = bf16[256,2048]{1,0:T(8,128)(2,1)} async-done(((bf16[1024,2048]{1,0:T(8,128)(2,1)}), bf16[256,2048]{1,0:T(8,128)(2,1)}) %reduce-scatter.14.cloned.1.call-update) | async-done | bytes 1048592 | tf_op jit(solution)/shard_map/reduce_scatter | solution.py:224
  (267 shorter events, 191.0 us)
Async XLA Ops:
  7.2 34.3 %all-gather.18.cloned.1.call-start = ((), (), s32[]{:S(2)}) async-start(), calls=%async_computation.14 | async-start | bytes 2359296 | tf_op jit(solution)/shard_map/all_gather | solution.py:185
  7.9 88.0 %all-gather.12.cloned.1.call-start = ((), (), s32[]{:S(2)}) async-start(), calls=%async_computation.11 | async-start | bytes 5242880 | tf_op jit(solution)/shard_map/all_gather | solution.py:194
  14.7 112.0 %all-gather.16.cloned.1.call-start = ((), (), s32[]{:S(2)}) async-start(), calls=%async_computation.13 | async-start | bytes 2359296 | tf_op jit(solution)/shard_map/all_gather | solution.py:184
  15.5 141.3 %all-gather.14.cloned.1.call-start = ((), (), s32[]{:S(2)}) async-start(), calls=%async_computation.12 | async-start | bytes 2359296 | tf_op jit(solution)/shard_map/all_gather | solution.py:186
  16.1 172.2 %all-gather.20.cloned.1.call-start = ((), (), s32[]{:S(2)}) async-start(), calls=%async_computation.15 | async-start | bytes 2359296 | tf_op jit(solution)/shard_map/all_gather | solution.py:187
  16.6 229.4 %reduce-scatter.12.cloned.1.call-start = ((), (), s32[]{:S(2)}) async-start(), calls=%async_computation.16 | async-start | bytes 5242880 | tf_op jit(solution)/shard_map/reduce_scatter | solution.py:211
  194.2 135.5 %all-gather.26.cloned.1.call-start = ((), (), s32[]{:S(2)}) async-start(), calls=%async_computation.19 | async-start | bytes 9437184 | tf_op jit(solution)/shard_map/all_gather | solution.py:189
  195.0 188.2 %all-gather.22.cloned.1.call-start = ((), (), s32[]{:S(2)}) async-start(), calls=%async_computation.17 | async-start | bytes 5242880 | tf_op jit(solution)/shard_map/all_gather | solution.py:219
  247.7 459.1 %copy-start.39 = (f32[256]{0:T(256)}, f32[256]{0:T(256)S(1)}, u32[]{:S(2)}) copy-start(f32[256]{0:T(256)S(1)} %broadcast_multiply_fusion) | copy-start | bytes 3076
  249.5 457.3 %copy-start.47 = (f32[256]{0:T(256)}, f32[256]{0:T(256)S(1)}, u32[]{:S(2)}) copy-start(f32[256]{0:T(256)S(1)} %fusion.101) | copy-start | bytes 3076
  250.9 215.9 %all-gather.24.cloned.1.call-start = ((), (), s32[]{:S(2)}) async-start(), calls=%async_computation.18 | async-start | bytes 9437184 | tf_op jit(solution)/shard_map/all_gather | solution.py:188
  251.7 268.6 %all-gather.30.cloned.1.call-start = ((), (), s32[]{:S(2)}) async-start(), calls=%async_computation.22 | async-start | bytes 5242880 | tf_op jit(solution)/shard_map/all_gather | solution.py:242
  253.1 453.8 %copy-start.53 = (f32[256]{0:T(256)}, f32[256]{0:T(256)S(1)}, u32[]{:S(2)}) copy-start(f32[256]{0:T(256)S(1)} %dynamic-slice_convert_fusion) | copy-start | bytes 3076
  254.3 350.1 %all-gather.28.cloned.1.call-start = ((), (), s32[]{:S(2)}) async-start(), calls=%async_computation.20 | async-start | bytes 9437184 | tf_op jit(solution)/shard_map/all_gather | solution.py:190
  255.0 447.8 %reduce-scatter.16.cloned.1.call-start = ((), (), s32[]{:S(2)}) async-start(), calls=%async_computation.23 | async-start | bytes 5242880 | tf_op jit(solution)/shard_map/reduce_scatter | solution.py:252
  651.9 110.2 %all-gather.32.cloned.1.call-start = ((), (), s32[]{:S(2)}) async-start(), calls=%async_computation.24 | async-start | bytes 5242880 | tf_op jit(solution)/shard_map/all_gather | solution.py:261
  709.4 200.5 %reduce-scatter.30.cloned.1.call-start = ((), (), s32[]{:S(2)}) async-start(), calls=%async_computation.31 | async-start | bytes 9437184 | tf_op jit(solution)/shard_map/reduce_scatter | solution.py:305
  723.8 220.2 %reduce-scatter.28.cloned.1.call-start = ((), (), s32[]{:S(2)}) async-start(), calls=%async_computation.30 | async-start | bytes 9437184 | tf_op jit(solution)/shard_map/reduce_scatter | solution.py:302
  738.0 296.2 %reduce-scatter.32.cloned.1.call-start = ((), (), s32[]{:S(2)}) async-start(), calls=%async_computation.32 | async-start | bytes 9437184 | tf_op jit(solution)/shard_map/reduce_scatter | solution.py:308
  752.4 318.4 %reduce-scatter.26.cloned.1.call-start = ((), (), s32[]{:S(2)}) async-start(), calls=%async_computation.29 | async-start | bytes 2359296 | tf_op jit(solution)/shard_map/reduce_scatter | solution.py:299
  768.0 339.7 %reduce-scatter.24.cloned.1.call-start = ((), (), s32[]{:S(2)}) async-start(), calls=%async_computation.28 | async-start | bytes 2359296 | tf_op jit(solution)/shard_map/reduce_scatter | solution.py:296
  784.3 360.4 %reduce-scatter.20.cloned.1.call-start = ((), (), s32[]{:S(2)}) async-start(), calls=%async_computation.26 | async-start | bytes 2359296 | tf_op jit(solution)/shard_map/reduce_scatter | solution.py:290
  875.6 305.9 %reduce-scatter.22.cloned.1.call-start = ((), (), s32[]{:S(2)}) async-start(), calls=%async_computation.27 | async-start | bytes 2359296 | tf_op jit(solution)/shard_map/reduce_scatter | solution.py:293
  884.7 351.0 %reduce-scatter.18.cloned.1.call-start = ((), (), s32[]{:S(2)}) async-start(), calls=%async_computation.25 | async-start | bytes 5242880 | tf_op jit(solution)/shard_map/reduce_scatter | solution.py:277
  895.5 395.8 %reduce-scatter.14.cloned.1.call-start = ((), (), s32[]{:S(2)}) async-start(), calls=%async_computation.21 | async-start | bytes 5242880 | tf_op jit(solution)/shard_map/reduce_scatter | solution.py:224
  912.7 323.0 %copy-start.1 = (bf16[256,2048]{1,0:T(8,128)(2,1)S(1)}, bf16[256,2048]{1,0:T(8,128)(2,1)}, u32[]{:S(2)}) copy-start(bf16[256,2048]{1,0:T(8,128)(2,1)} %param.22) | copy-start | bytes 3145732
  912.7 323.0 %copy-start.42 = (f32[256]{0:T(256)S(1)}, f32[256]{0:T(256)}, u32[]{:S(2)}) copy-start(f32[256]{0:T(256)} %copy-done.41) | copy-start | bytes 3076
  946.8 290.7 %copy-start.58 = (f32[256]{0:T(256)S(1)}, f32[256]{0:T(256)}, u32[]{:S(2)}) copy-start(f32[256]{0:T(256)} %copy-done.57) | copy-start | bytes 3076
  946.8 290.7 %copy-start.50 = (f32[256]{0:T(256)S(1)}, f32[256]{0:T(256)}, u32[]{:S(2)}) copy-start(f32[256]{0:T(256)} %copy-done.49) | copy-start | bytes 3076
  1036.9 254.5 %copy-start.52 = (f32[256]{0:T(256)S(1)}, f32[256]{0:T(256)}, u32[]{:S(2)}) copy-start(f32[256]{0:T(256)} %copy-done.51) | copy-start | bytes 3076
  1036.9 254.5 %copy-start.54 = (f32[256]{0:T(256)S(1)}, f32[256]{0:T(256)}, u32[]{:S(2)}) copy-start(f32[256]{0:T(256)} %copy-done.53) | copy-start | bytes 3076
  1036.9 254.5 %copy-start.56 = (f32[256]{0:T(256)S(1)}, f32[256]{0:T(256)}, u32[]{:S(2)}) copy-start(f32[256]{0:T(256)} %copy-done.55) | copy-start | bytes 3076
  (57 other events, 1466.1 us)
Sparse Core Ops, SparseCore 0:
  9.6 31.8 all-gather.17
  43.9 51.9 all-gather.11
  97.5 29.1 all-gather.15
  128.2 28.5 all-gather.13
  158.2 30.0 all-gather.19
  194.4 51.6 reduce-scatter.11
  247.6 82.0 all-gather.25
  332.1 51.0 all-gather.21
  384.8 82.0 all-gather.23
  469.2 51.0 all-gather.29
  521.8 82.4 all-gather.27
  652.0 50.7 reduce-scatter.15
  709.5 52.5 all-gather.31
  764.3 89.5 reduce-scatter.29
  856.0 87.9 reduce-scatter.27
  946.1 87.9 reduce-scatter.31
  1036.3 34.5 reduce-scatter.25
  1073.0 34.6 reduce-scatter.23
  1110.0 34.6 reduce-scatter.19
  1146.8 34.5 reduce-scatter.21
  1184.4 51.2 reduce-scatter.17
  1238.7 52.5 reduce-scatter.13
where the time goes:
time: 1310 us; the launch traced here: 1300 us
  waiting for transfers between devices  921 us (70%)
  matrix products  281 us (21%)
  other arithmetic  67.1 us (5%)
  local copies, waits for them, and re-layouts  16.4 us (1%)
  between operations  15.6 us (1%)
    reduce_scatter x1, waiting for transfers between devices, per_device(): lax.psum_scatter(down_part.astype(jnp.bfloat16), 'dp', scatter_dimension=...  87.4 us
    all_gather x1, waiting for transfers between devices, per_device(): lax.all_gather(down_weight, 'dp', axis=1, tiled=True)  84.1 us
    all_gather x1, waiting for transfers between devices, per_device(): lax.all_gather(up_weight, 'dp', axis=0, tiled=True)  74.6 us
    all_gather x1, waiting for transfers between devices, per_device(): lax.all_gather(gate_weight, 'dp', axis=0, tiled=True)  68.9 us
    dot_general x7, matrix products, dot_first(): lax.dot_general(left, right, (((0,), (0,)), ((), ())), preferred_element_...  65 us
    dot_general x7, matrix products, dot_last(): lax.dot_general(left, right, (((1,), (1,)), ((), ())), preferred_element_...  64.1 us
    all_gather x1, waiting for transfers between devices, per_device(): gathered_one = lax.all_gather(normed_one, 'tensor', axis=0, tiled=True)  54.4 us
    all_gather x1, waiting for transfers between devices, per_device(): gathered_two = lax.all_gather(normed_two, 'tensor', axis=0, tiled=True)  53.5 us
  transfers between devices with their start and end apart: 22, of which 21 were waited for; matrix products, arithmetic and copies ran while one was open for 23% of the time, Pallas kernels for 0%

commit v1 on v0

--- a/solution.py
+++ b/solution.py
@@ -9,6 +9,18 @@
 EPSILON = 1e-05
 ROPE_BASE = 10000.0
 MASKED = -1e30
+
+
+def collect(array, axis, dim):
+    ways, here = (lax.axis_size(axis), lax.axis_index(axis))
+    grown, reach = (array, 1)
+    while reach < ways:
+        theirs = lax.ppermute(grown, axis, [(d, d ^ reach) for d in range(ways)])
+        mine_first = jnp.concatenate([grown, theirs], axis=dim)
+        theirs_first = jnp.concatenate([theirs, grown], axis=dim)
+        grown = jnp.where(here & reach == 0, mine_first, theirs_first)
+        reach = 2 * reach
+    return grown
 
 
 def layer_norm(rows):
@@ -187,7 +199,7 @@
         lax.all_gather(output_weight, "dp", axis=1, tiled=True),
         lax.all_gather(gate_weight, "dp", axis=0, tiled=True),
         lax.all_gather(up_weight, "dp", axis=0, tiled=True),
-        lax.all_gather(down_weight, "dp", axis=1, tiled=True),
+        collect(down_weight, "dp", 1),
     )
     residual_in = tokens.astype(jnp.float32)
     normed_one = layer_norm(residual_in).astype(jnp.bfloat16)

time: 1310 us -> 1520 us (1.16)
  waiting for transfers between devices: 921 us -> 1110 us
    ppermute x0 -> x3, waiting for transfers between devices: none -> 342 us  [collect(): theirs = lax.ppermute(grown, axis, [(d, d ^ reach) for d in range(ways)])]
    reduce_scatter x1, waiting for transfers between devices: 87.4 us -> 0.01 us  [per_device(): lax.psum_scatter(down_part.astype(jnp.bfloat16), 'dp', scatter_dimension=...]
    reduce_scatter x1, waiting for transfers between devices: 35.1 us -> 0.38 us  [per_device(): lax.psum_scatter(value_local.astype(jnp.bfloat16), 'dp', scatter_dimensio...]
    reduce_scatter x1, waiting for transfers between devices: 31.3 us -> 0.02 us  [per_device(): lax.psum_scatter(gate_local.astype(jnp.bfloat16), 'dp', scatter_dimension...]
  transfers between devices with their start and end apart: 22 -> 25, of which waited for: 21 -> 22; matrix products, arithmetic and copies ran while one was open for 23% -> 21% of each run, Pallas kernels for 0% -> 0%
where the time goes in v1:
time: 1520 us; the launch traced here: 1510 us
  waiting for transfers between devices  1110 us (73%)
  matrix products  291 us (19%)
  other arithmetic  75.2 us (5%)
  local copies, waits for them, and re-layouts  16.2 us (1%)
  between operations  15.7 us (1%)
    ppermute x3, waiting for transfers between devices, collect(): theirs = lax.ppermute(grown, axis, [(d, d ^ reach) for d in range(ways)])  342 us
    all_gather x1, waiting for transfers between devices, per_device(): lax.all_gather(down_weight, 'dp', axis=1, tiled=True)  84.1 us
    all_gather x1, waiting for transfers between devices, per_device(): lax.all_gather(gate_weight, 'dp', axis=0, tiled=True)  74.6 us
    all_gather x1, waiting for transfers between devices, per_device(): lax.all_gather(up_weight, 'dp', axis=0, tiled=True)  69.1 us
    dot_general x7, matrix products, dot_last(): lax.dot_general(left, right, (((1,), (1,)), ((), ())), preferred_element_...  65.8 us
    dot_general x7, matrix products, dot_first(): lax.dot_general(left, right, (((0,), (0,)), ((), ())), preferred_element_...  65.2 us
    all_gather x1, waiting for transfers between devices, per_device(): gathered_one = lax.all_gather(normed_one, 'tensor', axis=0, tiled=True)  54.4 us
    all_gather x1, waiting for transfers between devices, per_device(): gathered_two = lax.all_gather(normed_two, 'tensor', axis=0, tiled=True)  53.5 us
  transfers between devices with their start and end apart: 25, of which 22 were waited for; matrix products, arithmetic and copies ran while one was open for 21% of the time, Pallas kernels for 0%

profile of v1, /device:TPU:0, one launch (start us, length us, event | category | flops | bytes accessed | tf_op | source)
XLA Modules:
  0.0 1513.4 jit_solution(12460206742772263865)
XLA Ops:
  22.0 19.6 %all-gather.16.cloned.1.call-done = bf16[2048,512]{1,0:T(8,128)(2,1)} async-done(((bf16[256,512]{1,0:T(8,128)(2,1)}), bf16[2048,512]{1,0:T(8,128)(2,1)}) %all-gather.16.cloned.1.call-update) | async-done | bytes 2097168 | tf_op jit(solution)/shard_map/all_gather | solution.py:196
  41.5 54.4 %all-gather.12.cloned.1.call-done = bf16[1024,2048]{1,0:T(8,128)(2,1)} async-done(((bf16[256,2048]{1,0:T(8,128)(2,1)}), bf16[1024,2048]{1,0:T(8,128)(2,1)}) %all-gather.12.cloned.1.call-update) | async-done | bytes 4194320 | tf_op jit(solution)/shard_map/all_gather | solution.py:206
  103.3 23.5 %all-gather.18.cloned.1.call-done = bf16[2048,512]{1,0:T(8,128)(2,1)} async-done(((bf16[256,512]{1,0:T(8,128)(2,1)}), bf16[2048,512]{1,0:T(8,128)(2,1)}) %all-gather.18.cloned.1.call-update) | async-done | bytes 2097168 | tf_op jit(solution)/shard_map/all_gather | solution.py:197
  145.4 11.4 all-gather.14.cloned.1.call-done
  174.5 13.8 all-gather.20.cloned.1.call-done
  195.0 51.0 %reduce-scatter.12.cloned.1.call-done = bf16[256,2048]{1,0:T(8,128)(2,1)} async-done(((bf16[1024,2048]{1,0:T(8,128)(2,1)}), bf16[256,2048]{1,0:T(8,128)(2,1)}) %reduce-scatter.12.cloned.1.call-update) | async-done | bytes 1048592 | tf_op jit(solution)/shard_map/reduce_scatter | solution.py:223
  255.1 74.6 %all-gather.24.cloned.1.call-done = bf16[2048,2048]{1,0:T(8,128)(2,1)} async-done(((bf16[256,2048]{1,0:T(8,128)(2,1)}), bf16[2048,2048]{1,0:T(8,128)(2,1)}) %all-gather.24.cloned.1.call-update) | async-done | bytes 8388624 | tf_op jit(solution)/shard_map/all_gather | solution.py:200
  329.7 53.5 %all-gather.22.cloned.1.call-done = bf16[1024,2048]{1,0:T(8,128)(2,1)} async-done(((bf16[256,2048]{1,0:T(8,128)(2,1)}), bf16[1024,2048]{1,0:T(8,128)(2,1)}) %all-gather.22.cloned.1.call-update) | async-done | bytes 4194320 | tf_op jit(solution)/shard_map/all_gather | solution.py:231
  383.3 14.6 fusion.141
  397.9 69.1 %all-gather.26.cloned.1.call-done = bf16[2048,2048]{1,0:T(8,128)(2,1)} async-done(((bf16[256,2048]{1,0:T(8,128)(2,1)}), bf16[2048,2048]{1,0:T(8,128)(2,1)}) %all-gather.26.cloned.1.call-update) | async-done | bytes 8388624 | tf_op jit(solution)/shard_map/all_gather | solution.py:201
  466.9 14.5 fusion.142
  481.4 38.9 %all-gather.28.cloned.1.call-done = bf16[1024,2048]{1,0:T(8,128)(2,1)} async-done(((bf16[256,2048]{1,0:T(8,128)(2,1)}), bf16[1024,2048]{1,0:T(8,128)(2,1)}) %all-gather.28.cloned.1.call-update) | async-done | bytes 4194320 | tf_op jit(solution)/shard_map/all_gather | solution.py:254
  520.3 84.1 %all-gather.30.cloned.1.call-done = bf16[2048,2048]{1,0:T(8,128)(2,1)} async-done(((bf16[2048,256]{1,0:T(8,128)(2,1)}), bf16[2048,2048]{1,0:T(8,128)(2,1)}) %all-gather.30.cloned.1.call-update) | async-done | bytes 8388624 | tf_op jit(solution)/shard_map/all_gather | solution.py:250
  604.4 21.7 %multiply_convert_fusion.1 = (bf16[1024,2048]{1,0:T(8,128)(2,1)}, bf16[1024,2048]{1,0:T(8,128)(2,1)}, bf16[1024,2048]{1,0:T(8,128)(2,1)}) fusion(f32[1024,2048]{1,0:T(8,128)} %fusion.141, f32[1024,2048]{1,0:T(8,128)} %fusion.142, bf16[1024,2048]{1,0:T(8,128)(2,1)} %all-gather.28.cloned.1.call-done, bf16[2048,2048]{1,0:T(8,128)(2,1)} %all-gather.30.cloned.1.call-done), kind=kOutput, calls=%fused_computation.19 | convolution fusion | flops 8623489024 | bytes 41943040 | tf_op jit(solution)/shard_map/dot_general | solution.py:79
  626.1 14.9 fusion.143
  641.0 12.2 add_convert_fusion.1
  653.2 50.9 %reduce-scatter.16.cloned.1.call-done = bf16[256,2048]{1,0:T(8,128)(2,1)} async-done(((bf16[1024,2048]{1,0:T(8,128)(2,1)}), bf16[256,2048]{1,0:T(8,128)(2,1)}) %reduce-scatter.16.cloned.1.call-update) | async-done | bytes 1048592 | tf_op jit(solution)/shard_map/reduce_scatter | solution.py:264
  710.7 14.5 convolution_convert_fusion.2
  725.2 14.1 convolution_convert_fusion.1
  739.4 14.2 convolution_convert_fusion
  785.4 9.3 fusion.94
  800.6 20.8 %fusion.97 = f32[512,4,128]{2,0,1:T(8,128)} fusion(f32[4,512,1024]{2,1,0:T(8,128)} %fusion.145, f32[4,512,1024]{2,1,0:T(8,128)} %copy-done.6, f32[4,512]{1,0:T(4,128)S(1)} %log_add_fusion, pred[512,1024]{1,0:T(8,128)(4,1)S(1)} %copy-done.20, bf16[1024,4,64]{2,0,1:T(8,128)(2,1)S(1)} %copy-done.13, bf16[1024,4,64]{2,0,1:T(8,128)(2,1)S(1)} %copy-done.11), kind=kOutput, calls=%fused_computation.123 | convolution fusion | flops 562039808 | bytes 19406848 | tf_op jit(solution)/shard_map/hqk,khd->qhd/dot_general | solution.py:153
  821.4 9.4 fusion.91
  830.8 26.4 %bitcast_add_fusion.1 = f32[1024,4,128]{2,0,1:T(8,128)} fusion(f32[512,4,128]{2,0,1:T(8,128)S(1)} %copy-done.66, bf16[512,4,128]{2,0,1:T(8,128)(2,1)S(1)} %copy-done.25, f32[4,512,1024]{2,1,0:T(8,128)} %fusion.145, f32[4,512,1024]{2,1,0:T(8,128)} %copy-done.6, f32[4,512]{1,0:T(4,128)S(1)} %log_add_fusion, pred[512,1024]{1,0:T(8,128)(4,1)S(1)} %copy-done.20), kind=kOutput, calls=%fused_computation.89 | convolution fusion | flops 560466944 | bytes 20979712 | tf_op jit(solution)/shard_map/hqk,qhd->khd/dot_general | solution.py:161
  908.3 79.2 %collective-permute-done.1 = bf16[2048,512]{1,0:T(8,128)(2,1)} collective-permute-done((bf16[2048,512]{1,0:T(8,128)(2,1)S(1)}, bf16[2048,512]{1,0:T(8,128)(2,1)}, u32[]{:S(2)}, u32[]{:S(2)}) %collective-permute-start.1) | collective-permute-done | bytes 2097184 | tf_op jit(solution)/shard_map/ppermute | solution.py:18
  994.6 259.6 %collective-permute-done.2 = bf16[2048,1024]{1,0:T(8,128)(2,1)} collective-permute-done((bf16[2048,1024]{1,0:T(8,128)(2,1)}, bf16[2048,1024]{1,0:T(8,128)(2,1)}, u32[]{:S(2)}, u32[]{:S(2)}) %collective-permute-start.2) | collective-permute-done | bytes 4194336 | tf_op jit(solution)/shard_map/ppermute | solution.py:18
  1254.2 18.1 %fusion.49 = bf16[1024,2048]{1,0:T(8,128)(2,1)} fusion(bf16[1024,2048]{1,0:T(8,128)(2,1)} %get-tuple-element.75, bf16[2048,1024]{1,0:T(8,128)(2,1)} %collective-permute-done.2, bf16[2048,1024]{1,0:T(8,128)(2,1)} %maximum_select_fusion.2, pred[]{:T(512)S(6)} %eq.79), kind=kOutput, calls=%fused_computation.57 | convolution fusion | flops 8629780480 | bytes 16777216 | tf_op jit(solution)/shard_map/dot_general | solution.py:237
  1283.2 35.2 %reduce-scatter.22.cloned.1.call-done = bf16[256,512]{1,0:T(8,128)(2,1)} async-done(((bf16[2048,512]{1,0:T(8,128)(2,1)}), bf16[256,512]{1,0:T(8,128)(2,1)}) %reduce-scatter.22.cloned.1.call-update) | async-done | bytes 262160 | tf_op jit(solution)/shard_map/reduce_scatter | solution.py:305
  1320.2 34.9 %reduce-scatter.26.cloned.1.call-done = bf16[512,256]{1,0:T(8,128)(2,1)} async-done(((bf16[512,2048]{1,0:T(8,128)(2,1)}), bf16[512,256]{1,0:T(8,128)(2,1)}) %reduce-scatter.26.cloned.1.call-update) | async-done | bytes 262160 | tf_op jit(solution)/shard_map/reduce_scatter | solution.py:311
  1356.9 35.0 %reduce-scatter.20.cloned.1.call-done = bf16[256,512]{1,0:T(8,128)(2,1)} async-done(((bf16[2048,512]{1,0:T(8,128)(2,1)}), bf16[256,512]{1,0:T(8,128)(2,1)}) %reduce-scatter.20.cloned.1.call-update) | async-done | bytes 262160 | tf_op jit(solution)/shard_map/reduce_scatter | solution.py:302
  1393.7 52.4 %reduce-scatter.18.cloned.1.call-done = bf16[256,2048]{1,0:T(8,128)(2,1)} async-done(((bf16[1024,2048]{1,0:T(8,128)(2,1)}), bf16[256,2048]{1,0:T(8,128)(2,1)}) %reduce-scatter.18.cloned.1.call-update) | async-done | bytes 1048592 | tf_op jit(solution)/shard_map/reduce_scatter | solution.py:289
  1449.8 51.9 %reduce-scatter.14.cloned.1.call-done = bf16[256,2048]{1,0:T(8,128)(2,1)} async-done(((bf16[1024,2048]{1,0:T(8,128)(2,1)}), bf16[256,2048]{1,0:T(8,128)(2,1)}) %reduce-scatter.14.cloned.1.call-update) | async-done | bytes 1048592 | tf_op jit(solution)/shard_map/reduce_scatter | solution.py:236
  (276 shorter events, 200.2 us)
Async XLA Ops:
  7.2 34.3 %all-gather.16.cloned.1.call-start = ((), (), s32[]{:S(2)}) async-start(), calls=%async_computation.13 | async-start | bytes 2359296 | tf_op jit(solution)/shard_map/all_gather | solution.py:196
  7.9 88.0 %all-gather.12.cloned.1.call-start = ((), (), s32[]{:S(2)}) async-start(), calls=%async_computation.11 | async-start | bytes 5242880 | tf_op jit(solution)/shard_map/all_gather | solution.py:206
  14.8 111.9 %all-gather.18.cloned.1.call-start = ((), (), s32[]{:S(2)}) async-start(), calls=%async_computation.14 | async-start | bytes 2359296 | tf_op jit(solution)/shard_map/all_gather | solution.py:197
  15.5 141.2 %all-gather.14.cloned.1.call-start = ((), (), s32[]{:S(2)}) async-start(), calls=%async_computation.12 | async-start | bytes 2359296 | tf_op jit(solution)/shard_map/all_gather | solution.py:198
  16.1 172.1 %all-gather.20.cloned.1.call-start = ((), (), s32[]{:S(2)}) async-start(), calls=%async_computation.15 | async-start | bytes 2359296 | tf_op jit(solution)/shard_map/all_gather | solution.py:199
  16.7 229.4 %reduce-scatter.12.cloned.1.call-start = ((), (), s32[]{:S(2)}) async-start(), calls=%async_computation.16 | async-start | bytes 5242880 | tf_op jit(solution)/shard_map/reduce_scatter | solution.py:223
  194.2 135.5 %all-gather.24.cloned.1.call-start = ((), (), s32[]{:S(2)}) async-start(), calls=%async_computation.18 | async-start | bytes 9437184 | tf_op jit(solution)/shard_map/all_gather | solution.py:200
  195.0 188.3 %all-gather.22.cloned.1.call-start = ((), (), s32[]{:S(2)}) async-start(), calls=%async_computation.17 | async-start | bytes 5242880 | tf_op jit(solution)/shard_map/all_gather | solution.py:231
  247.8 460.3 %copy-start.40 = (f32[256]{0:T(256)}, f32[256]{0:T(256)S(1)}, u32[]{:S(2)}) copy-start(f32[256]{0:T(256)S(1)} %broadcast_multiply_fusion) | copy-start | bytes 3076
  249.6 458.5 %copy-start.48 = (f32[256]{0:T(256)}, f32[256]{0:T(256)S(1)}, u32[]{:S(2)}) copy-start(f32[256]{0:T(256)S(1)} %fusion.109) | copy-start | bytes 3076
  251.0 215.9 %all-gather.26.cloned.1.call-start = ((), (), s32[]{:S(2)}) async-start(), calls=%async_computation.19 | async-start | bytes 9437184 | tf_op jit(solution)/shard_map/all_gather | solution.py:201
  251.8 268.5 %all-gather.28.cloned.1.call-start = ((), (), s32[]{:S(2)}) async-start(), calls=%async_computation.21 | async-start | bytes 5242880 | tf_op jit(solution)/shard_map/all_gather | solution.py:254
  253.1 455.0 %copy-start.54 = (f32[256]{0:T(256)}, f32[256]{0:T(256)S(1)}, u32[]{:S(2)}) copy-start(f32[256]{0:T(256)S(1)} %dynamic-slice_convert_fusion) | copy-start | bytes 3076
  254.4 350.0 %all-gather.30.cloned.1.call-start = ((), (), s32[]{:S(2)}) async-start(), calls=%async_computation.22 | async-start | bytes 9437184 | tf_op jit(solution)/shard_map/all_gather | solution.py:250
  255.1 449.0 %reduce-scatter.16.cloned.1.call-start = ((), (), s32[]{:S(2)}) async-start(), calls=%async_computation.23 | async-start | bytes 5242880 | tf_op jit(solution)/shard_map/reduce_scatter | solution.py:264
  653.2 110.2 %all-gather.32.cloned.1.call-start = ((), (), s32[]{:S(2)}) async-start(), calls=%async_computation.24 | async-start | bytes 5242880 | tf_op jit(solution)/shard_map/all_gather | solution.py:273
  710.6 561.7 %reduce-scatter.28.cloned.1.call-start = ((), (), s32[]{:S(2)}) async-start(), calls=%async_computation.30 | async-start | bytes 9437184 | tf_op jit(solution)/shard_map/reduce_scatter | solution.py:314
  725.2 550.0 %reduce-scatter.30.cloned.1.call-start = ((), (), s32[]{:S(2)}) async-start(), calls=%async_computation.31 | async-start | bytes 9437184 | tf_op jit(solution)/shard_map/reduce_scatter | solution.py:317
  739.4 538.7 %reduce-scatter.32.cloned.1.call-start = ((), (), s32[]{:S(2)}) async-start(), calls=%async_computation.32 | async-start | bytes 9437184 | tf_op jit(solution)/shard_map/reduce_scatter | solution.py:320
  753.7 527.5 %reduce-scatter.24.cloned.1.call-start = ((), (), s32[]{:S(2)}) async-start(), calls=%async_computation.28 | async-start | bytes 2359296 | tf_op jit(solution)/shard_map/reduce_scatter | solution.py:308
  781.0 537.4 %reduce-scatter.22.cloned.1.call-start = ((), (), s32[]{:S(2)}) async-start(), calls=%async_computation.27 | async-start | bytes 2359296 | tf_op jit(solution)/shard_map/reduce_scatter | solution.py:305
  872.8 482.4 %reduce-scatter.26.cloned.1.call-start = ((), (), s32[]{:S(2)}) async-start(), calls=%async_computation.29 | async-start | bytes 2359296 | tf_op jit(solution)/shard_map/reduce_scatter | solution.py:311
  878.7 513.2 %reduce-scatter.20.cloned.1.call-start = ((), (), s32[]{:S(2)}) async-start(), calls=%async_computation.26 | async-start | bytes 2359296 | tf_op jit(solution)/shard_map/reduce_scatter | solution.py:302
  887.9 558.2 %reduce-scatter.18.cloned.1.call-start = ((), (), s32[]{:S(2)}) async-start(), calls=%async_computation.25 | async-start | bytes 5242880 | tf_op jit(solution)/shard_map/reduce_scatter | solution.py:289
  888.2 3.0 collective-permute-start
  894.1 93.4 %collective-permute-start.1 = (bf16[2048,512]{1,0:T(8,128)(2,1)S(1)}, bf16[2048,512]{1,0:T(8,128)(2,1)}, u32[]{:S(2)}, u32[]{:S(2)}) collective-permute-start(bf16[2048,512]{1,0:T(8,128)(2,1)S(1)} %maximum_select_fusion.5), channel_id=1, source_target_pairs={{0,8},{4,12},{8,0},{12,4},{16,24},{20,28},{24,16},{28,20},{1,9},{5... | collective-permute-start | bytes 6291464 | tf_op jit(solution)/shard_map/ppermute | solution.py:18
  907.9 593.7 %reduce-scatter.14.cloned.1.call-start = ((), (), s32[]{:S(2)}) async-start(), calls=%async_computation.20 | async-start | bytes 5242880 | tf_op jit(solution)/shard_map/reduce_scatter | solution.py:236
  992.5 261.7 %collective-permute-start.2 = (bf16[2048,1024]{1,0:T(8,128)(2,1)}, bf16[2048,1024]{1,0:T(8,128)(2,1)}, u32[]{:S(2)}, u32[]{:S(2)}) collective-permute-start(bf16[2048,1024]{1,0:T(8,128)(2,1)} %maximum_select_fusion.2), channel_id=1, source_target_pairs={{0,16},{4,20},{8,24},{12,28},{16,0},{20,4},{24,8},{28,12},{1,17},{... | collective-permute-start | bytes 12582920 | tf_op jit(solution)/shard_map/ppermute | solution.py:18
  1280.7 221.0 %copy-start.49 = (f32[256]{0:T(256)S(1)}, f32[256]{0:T(256)}, u32[]{:S(2)}) copy-start(f32[256]{0:T(256)} %copy-done.48) | copy-start | bytes 3076
  1280.8 221.0 %copy-start.53 = (f32[256]{0:T(256)S(1)}, f32[256]{0:T(256)}, u32[]{:S(2)}) copy-start(f32[256]{0:T(256)} %copy-done.52) | copy-start | bytes 3076
  1280.8 221.0 %copy-start.55 = (f32[256]{0:T(256)S(1)}, f32[256]{0:T(256)}, u32[]{:S(2)}) copy-start(f32[256]{0:T(256)} %copy-done.54) | copy-start | bytes 3076
  1280.8 221.0 %copy-start.57 = (f32[256]{0:T(256)S(1)}, f32[256]{0:T(256)}, u32[]{:S(2)}) copy-start(f32[256]{0:T(256)} %copy-done.56) | copy-start | bytes 3076
  (61 other events, 1757.7 us)
Sparse Core Ops, SparseCore 0:
  9.6 31.8 all-gather.15
  43.9 51.9 all-gather.11
  97.5 29.1 all-gather.17
  128.2 28.5 all-gather.13
  158.2 30.0 all-gather.19
  194.4 51.6 reduce-scatter.11
  247.7 82.0 all-gather.23
  332.2 51.0 all-gather.21
  384.9 82.0 all-gather.25
  469.2 51.0 all-gather.27
  521.9 82.4 all-gather.29
  653.3 50.7 reduce-scatter.15
  710.8 52.5 all-gather.31
  765.5 89.5 reduce-scatter.27
  857.2 132.6 reduce-scatter.29
  992.1 211.1 reduce-scatter.31
  1205.4 75.7 reduce-scatter.23
  1283.3 35.0 reduce-scatter.21
  1320.7 34.3 reduce-scatter.25
  1357.3 34.5 reduce-scatter.19
  1394.9 51.1 reduce-scatter.17
  1449.1 52.5 reduce-scatter.13
